TPU v7x, 256 devices: a whole 4x4x8 slice. The times are simulated.
256 devices in a mesh: dp: 16 (over x_lo, y, core), mp: 8 (over z), side: 2 (over x_hi).
Axes of the slice: x: 4 (x_hi: 2, x_lo: 2; x = x_hi * 2 + x_lo), y: 4, z: 8, core: 2. Of those that a mesh axis runs over, the one named last changes fastest.
Arguments:
- tokens: bfloat16 [4096, 3072], P('dp', 'mp'), may hold values from -6 to 6
- up_weight: bfloat16 [2, 3072, 6144], P('side', 'dp', 'mp'), may hold values from -0.109375 to 0.109375
- down_weight: bfloat16 [2, 6144, 3072], P('side', 'mp', 'dp'), may hold values from -0.078125 to 0.078125
- mod_table: float32 [2, 50, 3, 3072], P('side'), may hold values from -3 to 3
- timesteps: int32 [16], P('dp'), may hold values from 0 to 49
- valid_counts: int32 [16], replicated, may hold values from 64 to 256, as said below
Outputs:
- block_out: bfloat16 [2, 4096, 3072], P('side', 'dp', 'mp')
- up_grads: float32 [3072, 6144], P(('dp', 'side'), 'mp')
- down_grads: float32 [6144, 3072], P('mp', ('dp', 'side'))
Inputs may be any that keep to these rules, and one draw needn't show every extreme that they name: `valid_counts`: every image has at least 64 valid tokens, and in every draw some image has all 256 valid.
All inputs are finite; a program needn't handle non-finite values.
Results may differ from a plain program's by a relative error of at most 0.018.
Values may be sent and summed in bfloat16 or wider, within the bound.
A program may use at most 64 MiB of HBM per device.

v0:
```python
import jax
import jax.numpy as jnp
from jax import lax
from jax.sharding import PartitionSpec as P


def passed_along(x, axis, by):
    peers = lax.axis_size(axis)
    pairs = [(i, i + by) for i in range(peers) if 0 <= i + by < peers]
    return lax.ppermute(x, axis, pairs)


def gelu_tanh(values):
    return jax.nn.gelu(values, approximate=True)


def shards(tokens, up_weight, down_weight, mod_table, timesteps, valid_counts):
    gathered = lax.all_gather(tokens, "mp", axis=1, tiled=True)
    width = gathered.shape[1]
    shard_width = tokens.shape[1]
    mp_offset = lax.axis_index("mp") * shard_width
    is_student = lax.axis_index("side") == 1
    wide = gathered.astype(jnp.float32)
    average = jnp.mean(wide, axis=-1, keepdims=True)
    centred = wide - average
    variance = jnp.mean(centred * centred, axis=-1, keepdims=True)
    scaled = centred * lax.rsqrt(variance + 1e-06)
    plan = mod_table.shape[1]
    one_hot = (jnp.arange(plan, dtype=jnp.int32)[None, :] == timesteps[0]).astype(jnp.float32)
    modulation = jnp.dot(
        one_hot,
        mod_table[0].reshape(plan, 3 * width),
        precision=lax.Precision.HIGHEST,
        preferred_element_type=jnp.float32,
    ).reshape(3, width)
    normed = (scaled * (1.0 + modulation[1]) + modulation[0]).astype(jnp.bfloat16)
    gate_row = modulation[2]
    hidden_pre = jnp.dot(
        normed,
        lax.all_gather(up_weight[0], "dp", axis=0, tiled=True),
        preferred_element_type=jnp.float32,
    )
    hidden_act = gelu_tanh(hidden_pre).astype(jnp.bfloat16)
    down_full = lax.all_gather(down_weight[0], "dp", axis=1, tiled=True)
    partial_value = jnp.dot(hidden_act, down_full, preferred_element_type=jnp.float32)
    positions = jnp.arange(normed.shape[0], dtype=jnp.int32)
    own_count = lax.dynamic_index_in_dim(valid_counts, lax.axis_index("dp"), 0, keepdims=False)
    valid_col = (positions < own_count).astype(jnp.float32)[:, None]
    valid_total = jnp.sum(valid_counts).astype(jnp.float32)
    mixed = lax.psum(partial_value.astype(jnp.bfloat16), "mp").astype(jnp.float32)
    out_full = (wide + gate_row * mixed).astype(jnp.bfloat16)
    out_local = lax.dynamic_slice_in_dim(out_full, mp_offset, shard_width, 1)
    other_full = passed_along(out_full, "side", 1)
    differ = out_full.astype(jnp.float32) - other_full.astype(jnp.float32)
    grad_out = (gate_row * differ * valid_col / jnp.sqrt(valid_total)).astype(jnp.bfloat16)

    def backprop():
        grad_act = lax.dot_general(
            grad_out, down_full, (((1,), (1,)), ((), ())), preferred_element_type=jnp.float32
        )
        unused, pullback = jax.vjp(gelu_tanh, hidden_pre)
        return pullback(grad_act)[0].astype(jnp.bfloat16)

    def no_backprop():
        return jnp.zeros(hidden_pre.shape, jnp.bfloat16)

    grad_pre = lax.cond(is_student, backprop, no_backprop)
    ff_width = hidden_act.shape[1]

    def product():
        return lax.dot_general(
            normed, grad_pre, (((0,), (0,)), ((), ())), preferred_element_type=jnp.float32
        )

    def nothing():
        return jnp.zeros(
            (width // lax.axis_size(("dp", "side")) * lax.axis_size(("dp", "side")), ff_width),
            jnp.float32,
        )

    up_share = lax.psum_scatter(
        lax.cond(is_student, product, nothing).astype(jnp.bfloat16),
        ("dp", "side"),
        scatter_dimension=0,
        tiled=True,
    ).astype(jnp.float32)

    def down_product():
        return lax.dot_general(
            hidden_act, grad_out, (((0,), (0,)), ((), ())), preferred_element_type=jnp.float32
        )

    def down_nothing():
        return jnp.zeros((ff_width, width), jnp.float32)

    down_term = lax.cond(is_student, down_product, down_nothing)
    down_share = lax.psum_scatter(
        down_term.astype(jnp.bfloat16), ("dp", "side"), scatter_dimension=1, tiled=True
    ).astype(jnp.float32)
    return (out_local[None], up_share, down_share)


def solution(mesh):
    placed = (
        P("dp", "mp"),
        P("side", "dp", "mp"),
        P("side", "mp", "dp"),
        P("side", None, None, None),
        P("dp"),
        P(),
    )
    return jax.shard_map(
        shards,
        mesh=mesh,
        in_specs=placed,
        out_specs=(P("side", "dp", "mp"), P(("dp", "side"), "mp"), P("mp", ("dp", "side"))),
        check_vma=False,
    )
```

profile of v0, /device:TPU:1, one launch (start us, length us, event | category | flops | bytes accessed | tf_op | source)
XLA Modules:
  0.0 593.4 jit_solution(2284106600337096998)
XLA Ops:
  7.2 0.0 all-gather.6.cloned.1.call-start
  7.2 0.7 all-gather.6.cloned.1.call-update
  7.9 0.0 all-gather.8.cloned.1.call-start
  7.9 0.7 all-gather.8.cloned.1.call-update
  8.6 0.0 all-gather.10.cloned.1.call-start
  8.7 0.7 all-gather.10.cloned.1.call-update
  9.4 0.0 all-reduce.2.cloned.1.call-start
  9.4 6.5 %reduce = f32[50,3,3072]{2,1,0:T(4,128)S(1)} reduce(f32[1,50,3,3072]{3,0,2,1:T(1,128)} %param.15, f32[]{:T(128)} %constant.65), dimensions={0}, to_apply=%param.15.reduce_sub_computation | reduce | bytes 3686404 | tf_op args[3]
  15.9 0.5 pad
  16.5 1.2 copy.14
  18.3 0.8 fusion.24
  19.1 29.2 %all-gather.6.cloned.1.call-done = bf16[256,3072]{1,0:T(8,128)(2,1)} async-done(((bf16[256,384]{1,0:T(8,128)(2,1)}), bf16[256,3072]{1,0:T(8,128)(2,1)}) %all-gather.6.cloned.1.call-update) | async-done | bytes 1572880 | tf_op jit(solution)/shard_map/all_gather | solution.py:18
  48.2 0.0 copy-start
  48.2 1.8 convert_reduce_fusion
  50.1 2.0 fusion.11
  52.0 0.0 copy-done
  52.0 0.8 fusion.14
  52.8 41.7 %all-gather.8.cloned.1.call-done = bf16[1,3072,768]{2,1,0:T(8,128)(2,1)} async-done(((bf16[1,192,768]{2,1,0:T(8,128)(2,1)}), bf16[1,3072,768]{2,1,0:T(8,128)(2,1)}) %all-gather.8.cloned.1.call-update) | async-done | bytes 4718608 | tf_op jit(solution)/shard_map/all_gather | solution.py:40
  94.5 4.6 fusion.23
  99.2 0.0 copy-start.1
  99.2 37.7 %all-gather.10.cloned.1.call-done = bf16[1,768,3072]{1,2,0:T(8,128)(2,1)} async-done(((bf16[1,768,192]{1,2,0:T(8,128)(2,1)}), bf16[1,768,3072]{1,2,0:T(8,128)(2,1)}) %all-gather.10.cloned.1.call-update) | async-done | bytes 4718608 | tf_op jit(solution)/shard_map/all_gather | solution.py:44
  136.9 4.9 convolution_convert_fusion
  141.8 0.0 copy-done.1
  141.8 0.0 copy-start.3
  141.8 0.0 all-reduce.2.cloned.1.call-update
  141.8 0.2 reduce-scatter.3.cloned.1.call-start
  142.1 74.3 %all-reduce.2.cloned.1.call-done = bf16[256,3072]{1,0:T(8,128)(2,1)} async-done(((bf16[256,3072]{1,0:T(8,128)(2,1)}), bf16[256,3072]{1,0:T(8,128)(2,1)}) %all-reduce.2.cloned.1.call-update) | async-done | bytes 1572880 | tf_op jit(solution)/shard_map/psum | solution.py:50
  216.3 3.1 fusion.15
  219.5 5.8 collective-permute-start
  225.2 0.0 copy-done.3
  225.2 0.6 reduce_sum.29
  226.6 0.6 dynamic_slice.8
  227.2 0.6 compare_convert_fusion
  227.8 25.6 %collective-permute-done = bf16[256,3072]{1,0:T(8,128)(2,1)} collective-permute-done((bf16[256,3072]{1,0:T(8,128)(2,1)}, bf16[256,3072]{1,0:T(8,128)(2,1)}, u32[]{:S(2)}, u32[]{:S(2)}) %collective-permute-start) | collective-permute-done | bytes 1572896 | tf_op jit(solution)/shard_map/ppermute | solution.py:10
  253.4 2.6 divide_convert_fusion
  256.0 0.1 conditional.3
  256.1 2.5 conditional.4
  256.1 2.5 broadcast.75
  258.6 0.0 copy-start.2
  258.6 0.0 reduce-scatter.3.cloned.1.call-update
  258.6 0.0 reduce-scatter.5.cloned.1.call-start
  258.6 0.9 copy-done.2
  259.6 2.8 conditional.5
  259.6 2.8 broadcast.76
  262.4 6.6 %copy.12 = bf16[768,3072]{0,1:T(8,128)(2,1)} copy(bf16[768,3072]{1,0:T(8,128)(2,1)} %get-tuple-element.43) | data formatting | bytes 9437184 | tf_op jit(solution)/shard_map/cond | solution.py:96
  269.0 0.0 reduce-scatter.5.cloned.1.call-update
  269.0 1.6 dynamic-slice_bitcast_fusion
  270.6 155.2 %reduce-scatter.3.cloned.1.call-done = bf16[96,768]{1,0:T(8,128)(2,1)} async-done(((bf16[3072,768]{1,0:T(8,128)(2,1)}), bf16[96,768]{1,0:T(8,128)(2,1)}) %reduce-scatter.3.cloned.1.call-update) | async-done | bytes 147472 | tf_op jit(solution)/shard_map/reduce_scatter | solution.py:81
  425.9 1.6 convert_element_type.71
  427.5 157.4 %reduce-scatter.5.cloned.1.call-done = bf16[768,96]{0,1:T(8,128)(2,1)} async-done(((bf16[768,3072]{0,1:T(8,128)(2,1)}), bf16[768,96]{0,1:T(8,128)(2,1)}) %reduce-scatter.5.cloned.1.call-update) | async-done | bytes 147472 | tf_op jit(solution)/shard_map/reduce_scatter | solution.py:97
  584.9 1.6 convert_element_type.73
  (4 shorter events, 0.1 us)
Async XLA Ops:
  7.2 41.1 %all-gather.6.cloned.1.call-start = ((), (), s32[]{:S(2)}) async-start(), calls=%async_computation.2 | async-start | bytes 1769472 | tf_op jit(solution)/shard_map/all_gather | solution.py:18
  7.9 86.6 %all-gather.8.cloned.1.call-start = ((), (), s32[]{:S(2)}) async-start(), calls=%async_computation.6 | async-start | bytes 5013504 | tf_op jit(solution)/shard_map/all_gather | solution.py:40
  8.6 128.2 %all-gather.10.cloned.1.call-start = ((), (), s32[]{:S(2)}) async-start(), calls=%async_computation.7 | async-start | bytes 5013504 | tf_op jit(solution)/shard_map/all_gather | solution.py:44
  9.4 207.0 %all-reduce.2.cloned.1.call-start = ((), (), s32[]{:S(2)}) async-start(), calls=%async_computation.3 | async-start | bytes 3145728 | tf_op jit(solution)/shard_map/psum | solution.py:50
  48.2 3.8 copy-start
  99.2 42.7 %copy-start.1 = (bf16[256,768]{1,0:T(8,128)(2,1)}, bf16[256,768]{1,0:T(8,128)(2,1)S(1)}, u32[]{:S(2)}) copy-start(bf16[256,768]{1,0:T(8,128)(2,1)S(1)} %get-tuple-element.39) | copy-start | bytes 1179652
  141.8 83.4 %copy-start.3 = (s32[16]{0:T(128)S(1)}, s32[16]{0:T(128)}, u32[]{:S(2)}) copy-start(s32[16]{0:T(128)} %param.17) | copy-start | bytes 196
  141.8 284.0 %reduce-scatter.3.cloned.1.call-start = ((), (), s32[]{:S(2)}) async-start(), calls=%async_computation.4 | async-start | bytes 4866048 | tf_op jit(solution)/shard_map/reduce_scatter | solution.py:81
  219.5 34.0 %collective-permute-start = (bf16[256,3072]{1,0:T(8,128)(2,1)}, bf16[256,3072]{1,0:T(8,128)(2,1)}, u32[]{:S(2)}, u32[]{:S(2)}) collective-permute-start(bf16[256,3072]{1,0:T(8,128)(2,1)} %fusion.15), channel_id=1, source_target_pairs={{0,1},{2,3},{4,5},{6,7},{8,9},{10,11},{12,13},{14,15},{16,17},{18,... | collective-permute-start | bytes 4718600 | tf_op jit(solution)/shard_map/ppermute | solution.py:10
  258.6 1.0 copy-start.2
  258.6 326.3 %reduce-scatter.5.cloned.1.call-start = ((), (), s32[]{:S(2)}) async-start(), calls=%async_computation.5 | async-start | bytes 4866048 | tf_op jit(solution)/shard_map/reduce_scatter | solution.py:97
Sparse Core Ops, SparseCore 0:
  9.8 38.4 all-gather.5
  50.1 44.3 all-gather.7
  96.4 40.4 all-gather.9
  142.0 74.3 all-reduce.1
  258.7 167.0 reduce-scatter.2
  428.2 156.6 reduce-scatter.4
where the time goes:
time: 594 us; the launch traced here: 593 us
  waiting for transfers between devices  523 us (88%)
  other arithmetic  21.3 us (4%)
  local copies, waits for them, and re-layouts  16.8 us (3%)
  between operations  15.5 us (3%)
  matrix products  10.3 us (2%)
  starting transfers between devices  6.19 us (1%)
    reduce_scatter x1, waiting for transfers between devices, shards(): lax.psum_scatter(down_term.astype(jnp.bfloat16), ('dp', 'side'), scatter_...  157 us
    reduce_scatter x1, waiting for transfers between devices, shards(): lax.psum_scatter(lax.cond(is_student, product, nothing).astype(jnp.bfloat...  155 us
    psum x1, waiting for transfers between devices, shards(): lax.psum(partial_value.astype(jnp.bfloat16), 'mp').astype(jnp.float32)  74.3 us
    all_gather x1, waiting for transfers between devices, shards(): lax.all_gather(up_weight[0], 'dp', axis=0, tiled=True)  41.7 us
    all_gather x1, waiting for transfers between devices, shards(): down_full = lax.all_gather(down_weight[0], 'dp', axis=1, tiled=True)  37.7 us
    all_gather x1, waiting for transfers between devices, shards(): gathered = lax.all_gather(tokens, 'mp', axis=1, tiled=True)  29.2 us
    ppermute x1, waiting for transfers between devices, passed_along(): return lax.ppermute(x, axis, pairs)  25.6 us
  transfers between devices with their start and end apart: 7, of which 7 were waited for; matrix products, arithmetic and copies ran while one was open for 6% of the time, Pallas kernels for 0%

commit v1 on v0

--- a/solution.py
+++ b/solution.py
@@ -2,6 +2,13 @@
 import jax.numpy as jnp
 from jax import lax
 from jax.sharding import PartitionSpec as P
+
+
+def all_by_exchange(shard, mesh_axis, dim):
+    size = lax.axis_size(mesh_axis)
+    pieces = jnp.stack([shard for _ in range(size)])
+    pieces = lax.all_to_all(pieces, mesh_axis, split_axis=0, concat_axis=0)
+    return jnp.concatenate(pieces, axis=dim)
 
 
 def passed_along(x, axis, by):
@@ -36,9 +43,7 @@
     normed = (scaled * (1.0 + modulation[1]) + modulation[0]).astype(jnp.bfloat16)
     gate_row = modulation[2]
     hidden_pre = jnp.dot(
-        normed,
-        lax.all_gather(up_weight[0], "dp", axis=0, tiled=True),
-        preferred_element_type=jnp.float32,
+        normed, all_by_exchange(up_weight[0], "dp", 0), preferred_element_type=jnp.float32
     )
     hidden_act = gelu_tanh(hidden_pre).astype(jnp.bfloat16)
     down_full = lax.all_gather(down_weight[0], "dp", axis=1, tiled=True)

time: 594 us -> 566 us (0.953)
  waiting for transfers between devices: 523 us -> 484 us
  starting transfers between devices: 6.19 us -> 13.6 us
    all_gather x1 -> x0, waiting for transfers between devices: 41.7 us -> none  [shards(): lax.all_gather(up_weight[0], 'dp', axis=0, tiled=True)]
    all_to_all x0 -> x1, waiting for transfers between devices: none -> 40 us  [all_by_exchange(): pieces = lax.all_to_all(pieces, mesh_axis, split_axis=0, concat_axis=0)]
    all_gather x1, waiting for transfers between devices: 37.7 us -> 8.62 us  [shards(): down_full = lax.all_gather(down_weight[0], 'dp', axis=1, tiled=True)]
    all_gather x1, waiting for transfers between devices: 29.2 us -> 19.7 us  [shards(): gathered = lax.all_gather(tokens, 'mp', axis=1, tiled=True)]
    all_to_all x0 -> x1, starting transfers between devices: none -> 7.51 us  [all_by_exchange(): pieces = lax.all_to_all(pieces, mesh_axis, split_axis=0, concat_axis=0)]
where the time goes in v1:
time: 566 us; the launch traced here: 565 us
  waiting for transfers between devices  484 us (86%)
  other arithmetic  21.4 us (4%)
  local copies, waits for them, and re-layouts  20.4 us (4%)
  between operations  15.2 us (3%)
  starting transfers between devices  13.6 us (2%)
  matrix products  10.4 us (2%)
    reduce_scatter x1, waiting for transfers between devices, shards(): lax.psum_scatter(down_term.astype(jnp.bfloat16), ('dp', 'side'), scatter_...  158 us
    reduce_scatter x1, waiting for transfers between devices, shards(): lax.psum_scatter(lax.cond(is_student, product, nothing).astype(jnp.bfloat...  156 us
    psum x1, waiting for transfers between devices, shards(): lax.psum(partial_value.astype(jnp.bfloat16), 'mp').astype(jnp.float32)  75.6 us
    all_to_all x1, waiting for transfers between devices, all_by_exchange(): pieces = lax.all_to_all(pieces, mesh_axis, split_axis=0, concat_axis=0)  40 us
    ppermute x1, waiting for transfers between devices, passed_along(): return lax.ppermute(x, axis, pairs)  25.6 us
    all_gather x1, waiting for transfers between devices, shards(): gathered = lax.all_gather(tokens, 'mp', axis=1, tiled=True)  19.7 us
  transfers between devices with their start and end apart: 7, of which 7 were waited for; matrix products, arithmetic and copies ran while one was open for 6% of the time, Pallas kernels for 0%

profile of v1, /device:TPU:1, one launch (start us, length us, event | category | flops | bytes accessed | tf_op | source)
XLA Modules:
  0.0 565.5 jit_solution(12662003448927047458)
XLA Ops:
  7.2 0.0 all-gather.4.cloned.1.call-start
  7.2 0.7 all-gather.4.cloned.1.call-update
  7.9 0.0 all-gather.6.cloned.1.call-start
  7.9 0.7 all-gather.6.cloned.1.call-update
  8.6 3.6 stack.3
  12.3 7.5 %all-to-all-start = ((bf16[16,192,768]{2,1,0:T(8,128)(2,1)}), bf16[16,192,768]{2,1,0:T(8,128)(2,1)}, u32[]{:S(2)}, u32[]{:S(2)}) async-start(bf16[16,192,768]{2,1,0:T(8,128)(2,1)} %stack.3), calls=%async_computation | async-start | bytes 9437184 | tf_op jit(solution)/shard_map/all_to_all | solution.py:10
  19.8 0.0 all-reduce.2.cloned.1.call-start
  19.8 6.5 %reduce = f32[50,3,3072]{2,1,0:T(4,128)S(1)} reduce(f32[1,50,3,3072]{3,0,2,1:T(1,128)} %param.15, f32[]{:T(128)} %constant.65), dimensions={0}, to_apply=%param.15.reduce_sub_computation | reduce | bytes 3686404 | tf_op args[3]
  26.4 0.5 pad
  26.9 1.2 copy.14
  28.7 0.8 fusion.22
  29.5 19.7 %all-gather.4.cloned.1.call-done = bf16[256,3072]{1,0:T(8,128)(2,1)} async-done(((bf16[256,384]{1,0:T(8,128)(2,1)}), bf16[256,3072]{1,0:T(8,128)(2,1)}) %all-gather.4.cloned.1.call-update) | async-done | bytes 1572880 | tf_op jit(solution)/shard_map/all_gather | solution.py:25
  49.2 0.0 copy-start
  49.2 1.8 convert_reduce_fusion
  51.0 2.0 fusion.9
  53.0 0.0 copy-done
  53.0 0.8 fusion.12
  53.8 40.0 %all-to-all-done = bf16[16,192,768]{2,1,0:T(8,128)(2,1)} async-done(((bf16[16,192,768]{2,1,0:T(8,128)(2,1)}), bf16[16,192,768]{2,1,0:T(8,128)(2,1)}, u32[]{:S(2)}, u32[]{:S(2)}) %all-to-all-start) | async-done | bytes 4718624 | tf_op jit(solution)/shard_map/all_to_all | solution.py:10
  93.8 4.7 fusion.21
  98.4 0.0 copy-start.1
  98.4 8.6 %all-gather.6.cloned.1.call-done = bf16[1,768,3072]{1,2,0:T(8,128)(2,1)} async-done(((bf16[1,768,192]{1,2,0:T(8,128)(2,1)}), bf16[1,768,3072]{1,2,0:T(8,128)(2,1)}) %all-gather.6.cloned.1.call-update) | async-done | bytes 4718608 | tf_op jit(solution)/shard_map/all_gather | solution.py:49
  107.1 4.9 convolution_convert_fusion
  112.0 0.0 copy-done.1
  112.0 0.0 copy-start.3
  112.0 0.0 all-reduce.2.cloned.1.call-update
  112.0 0.2 reduce-scatter.3.cloned.1.call-start
  112.2 75.6 %all-reduce.2.cloned.1.call-done = bf16[256,3072]{1,0:T(8,128)(2,1)} async-done(((bf16[256,3072]{1,0:T(8,128)(2,1)}), bf16[256,3072]{1,0:T(8,128)(2,1)}) %all-reduce.2.cloned.1.call-update) | async-done | bytes 1572880 | tf_op jit(solution)/shard_map/psum | solution.py:55
  187.9 3.1 fusion.13
  191.0 5.8 %collective-permute-start = (bf16[256,3072]{1,0:T(8,128)(2,1)}, bf16[256,3072]{1,0:T(8,128)(2,1)}, u32[]{:S(2)}, u32[]{:S(2)}) collective-permute-start(bf16[256,3072]{1,0:T(8,128)(2,1)} %fusion.13), channel_id=1, source_target_pairs={{0,1},{2,3},{4,5},{6,7},{8,9},{10,11},{12,13},{14,15},{16,17},{18,... | collective-permute-start | bytes 4718600 | tf_op jit(solution)/shard_map/ppermute | solution.py:17
  196.8 0.0 copy-done.3
  196.8 0.6 reduce_sum.29
  198.1 0.6 dynamic_slice.8
  198.7 0.6 compare_convert_fusion
  199.3 25.6 %collective-permute-done = bf16[256,3072]{1,0:T(8,128)(2,1)} collective-permute-done((bf16[256,3072]{1,0:T(8,128)(2,1)}, bf16[256,3072]{1,0:T(8,128)(2,1)}, u32[]{:S(2)}, u32[]{:S(2)}) %collective-permute-start) | collective-permute-done | bytes 1572896 | tf_op jit(solution)/shard_map/ppermute | solution.py:17
  225.0 2.6 divide_convert_fusion
  227.5 0.1 conditional.3
  227.6 2.5 conditional.4
  227.6 2.5 broadcast.76
  230.1 0.0 copy-start.2
  230.1 0.0 reduce-scatter.3.cloned.1.call-update
  230.1 0.0 reduce-scatter.5.cloned.1.call-start
  230.2 0.9 copy-done.2
  231.1 2.8 conditional.5
  231.1 2.8 broadcast.77
  233.9 6.6 %copy.12 = bf16[768,3072]{0,1:T(8,128)(2,1)} copy(bf16[768,3072]{1,0:T(8,128)(2,1)} %get-tuple-element.43) | data formatting | bytes 9437184 | tf_op jit(solution)/shard_map/cond | solution.py:101
  240.5 0.0 reduce-scatter.5.cloned.1.call-update
  240.5 1.6 dynamic-slice_bitcast_fusion
  242.2 155.5 %reduce-scatter.3.cloned.1.call-done = bf16[96,768]{1,0:T(8,128)(2,1)} async-done(((bf16[3072,768]{1,0:T(8,128)(2,1)}), bf16[96,768]{1,0:T(8,128)(2,1)}) %reduce-scatter.3.cloned.1.call-update) | async-done | bytes 147472 | tf_op jit(solution)/shard_map/reduce_scatter | solution.py:86
  397.7 1.6 convert_element_type.71
  399.3 158.0 %reduce-scatter.5.cloned.1.call-done = bf16[768,96]{0,1:T(8,128)(2,1)} async-done(((bf16[768,3072]{0,1:T(8,128)(2,1)}), bf16[768,96]{0,1:T(8,128)(2,1)}) %reduce-scatter.5.cloned.1.call-update) | async-done | bytes 147472 | tf_op jit(solution)/shard_map/reduce_scatter | solution.py:102
  557.3 1.6 convert_element_type.73
  (4 shorter events, 0.1 us)
Async XLA Ops:
  7.2 42.0 %all-gather.4.cloned.1.call-start = ((), (), s32[]{:S(2)}) async-start(), calls=%async_computation.3 | async-start | bytes 1769472 | tf_op jit(solution)/shard_map/all_gather | solution.py:25
  7.9 99.2 %all-gather.6.cloned.1.call-start = ((), (), s32[]{:S(2)}) async-start(), calls=%async_computation.7 | async-start | bytes 5013504 | tf_op jit(solution)/shard_map/all_gather | solution.py:49
  12.3 81.5 %all-to-all-start = ((bf16[16,192,768]{2,1,0:T(8,128)(2,1)}), bf16[16,192,768]{2,1,0:T(8,128)(2,1)}, u32[]{:S(2)}, u32[]{:S(2)}) async-start(bf16[16,192,768]{2,1,0:T(8,128)(2,1)} %stack.3), calls=%async_computation | async-start | bytes 9437184 | tf_op jit(solution)/shard_map/all_to_all | solution.py:10
  19.8 168.1 %all-reduce.2.cloned.1.call-start = ((), (), s32[]{:S(2)}) async-start(), calls=%async_computation.4 | async-start | bytes 3145728 | tf_op jit(solution)/shard_map/psum | solution.py:55
  49.2 3.8 copy-start
  98.4 13.5 %copy-start.1 = (bf16[256,768]{1,0:T(8,128)(2,1)}, bf16[256,768]{1,0:T(8,128)(2,1)S(1)}, u32[]{:S(2)}) copy-start(bf16[256,768]{1,0:T(8,128)(2,1)S(1)} %get-tuple-element.39) | copy-start | bytes 1179652
  112.0 84.8 %copy-start.3 = (s32[16]{0:T(128)S(1)}, s32[16]{0:T(128)}, u32[]{:S(2)}) copy-start(s32[16]{0:T(128)} %param.17) | copy-start | bytes 196
  112.0 285.7 %reduce-scatter.3.cloned.1.call-start = ((), (), s32[]{:S(2)}) async-start(), calls=%async_computation.5 | async-start | bytes 4866048 | tf_op jit(solution)/shard_map/reduce_scatter | solution.py:86
  191.0 34.0 %collective-permute-start = (bf16[256,3072]{1,0:T(8,128)(2,1)}, bf16[256,3072]{1,0:T(8,128)(2,1)}, u32[]{:S(2)}, u32[]{:S(2)}) collective-permute-start(bf16[256,3072]{1,0:T(8,128)(2,1)} %fusion.13), channel_id=1, source_target_pairs={{0,1},{2,3},{4,5},{6,7},{8,9},{10,11},{12,13},{14,15},{16,17},{18,... | collective-permute-start | bytes 4718600 | tf_op jit(solution)/shard_map/ppermute | solution.py:17
  230.1 1.0 copy-start.2
  230.1 327.2 %reduce-scatter.5.cloned.1.call-start = ((), (), s32[]{:S(2)}) async-start(), calls=%async_computation.6 | async-start | bytes 4866048 | tf_op jit(solution)/shard_map/reduce_scatter | solution.py:102
Sparse Core Ops, SparseCore 0:
  9.8 39.3 all-gather.3
  51.0 56.0 all-gather.5
  112.1 75.7 all-reduce.1
  230.2 167.4 reduce-scatter.2
  400.1 157.1 reduce-scatter.4
